TPU v7x, 512 devices: a whole 4x4x16 slice. The times are simulated.
512 devices in a mesh: grp: 32 (over y, z_lo), tp: 16 (over z_hi, x, core).
Axes of the slice: x: 4, y: 4, z: 16 (z_hi: 2, z_lo: 8; z = z_hi * 8 + z_lo), core: 2. Of those that a mesh axis runs over, the one named last changes fastest.
Arguments:
- tokens: bfloat16 [65536, 1536], P(('grp', 'tp')), may hold values from -6 to 6
- attn_gain: float32 [1536], replicated, may hold values from 0.1 to 1.9
- ffn_gain: float32 [1536], replicated, may hold values from 0.1 to 1.9
- w_query: bfloat16 [1536, 1024], P(None, 'tp')
- key_value_weight: bfloat16 [1536, 1024], P(None, 'tp'), may hold values from -0.15625 to 0.15625
- w_out: bfloat16 [1024, 1536], P('tp'), may hold values from -0.1875 to 0.1875
- segment_ids: int32 [65536], P(('grp', 'tp')), may hold values from 0 to 65535, as said below
- expert_ids: int32 [65536, 2], P(('grp', 'tp')), may hold values from 0 to 7, all different within a row; in each aligned block of 128 rows (0 to 127, 128 to 255, ...) at most 48 rows name the same one
- route_weights: float32 [65536, 2], P(('grp', 'tp')), may hold values from 0.2 to 1
- w_gate: bfloat16 [1536, 4096], P(None, 'tp'), may hold values from -0.15625 to 0.15625
- w_up: bfloat16 [1536, 4096], P(None, 'tp'), may hold values from -0.15625 to 0.15625
- w_down: bfloat16 [4096, 1536], P('tp'), may hold values from -0.25 to 0.25
- page_table: int32 [32, 128], P('grp'), may hold values from 0 to 127, each once within a row
Outputs:
- hidden_out: bfloat16 [65536, 1536], P(('grp', 'tp'))
- kv_cache: bfloat16 [4096, 16, 1024], P(('grp', 'tp'))
Inputs may be any that keep to these rules, and one draw needn't show every extreme that they name: `segment_ids`: each token's number is the stream position of its prompt's first token, so numbers never fall along the stream; a prompt covers at most 1024 tokens and some prompt exactly 1024; a prompt runs from every group into the next; the last token of the stream is a prompt of its own. `expert_ids`: in the tokens of one device no expert is named more than 48 times; in some device's tokens one expert is named exactly 48 times. `page_table`: each row names every page of the group once.
All inputs are finite; a program needn't handle non-finite values.
Results may differ from a plain program's by a relative error of at most 0.015.
The roundings to bfloat16 on the way count: a program that leaves them out, or rounds other values in their place, can miss the bound.
Values may be sent and summed in bfloat16 or wider, within the bound.
No kernel may reach another device: no remote copies, remote signals or barrier semaphores. Data moves between devices by JAX's collectives and lax.ppermute only.
A program may use at most 64 MiB of HBM per device.

v0:
```python
import functools
import jax
import jax.numpy as jnp
import numpy as np
from jax import lax
from jax.sharding import Mesh
from jax.sharding import PartitionSpec as P

AXES = ("y", "zl", "zh", "x", "c")
SIZES = (4, 8, 2, 4, 2)
ROW = ("x", "c")
PAGE = 16
CAP = 48


def permute(block, target):
    route = []
    for source in range(int(np.prod(SIZES))):
        place = dict(zip(AXES, (int(v) for v in np.unravel_index(source, SIZES))))
        goal = target(**place)
        if goal is not None:
            route.append((source, int(np.ravel_multi_index(goal, SIZES))))
    return lax.ppermute(block, AXES, route)


def swap_core(block):
    return permute(block, lambda y, zl, zh, x, c: (y, zl, zh, x, 1 - c))


def swap_half(block):
    return permute(block, lambda y, zl, zh, x, c: (y, zl, 1 - zh, x, c))


def swap_near(block):
    return permute(block, lambda y, zl, zh, x, c: (y, zl ^ 1, zh, x, c))


def next_group(block):

    def target(y, zl, zh, x, c):
        g = y * 8 + zl + 1
        return (g // 8, g % 8, zh, x, c) if zh == 0 and g < 32 else None

    return permute(block, target)


def ahead_x(block, step):
    return permute(block, lambda y, zl, zh, x, c: (y, zl, zh, (x - step) % 4, c))


def ahead_y(block, step):
    return permute(block, lambda y, zl, zh, x, c: ((y - step) % 4, zl, zh, x, c))


def from_all(block, ahead):
    one, three, two = [ahead(block, step) for step in (1, 3, 2)]
    return jnp.stack([block, one, two, three])


def in_order(relative, me):
    twice = jnp.concatenate([relative, relative], axis=0)
    return lax.dynamic_slice_in_dim(twice, (4 - me) % 4, 4, 0)


def rms_scale(row_data, gain_vec):
    values = row_data.astype(jnp.float32)
    inverse = lax.rsqrt(jnp.mean(values * values, axis=-1, keepdims=True) + 1e-05)
    return (values * inverse * gain_vec).astype(jnp.bfloat16)


def attend(queries, key_cat, value_cat, first_key, block_rows):
    rows = queries.shape[1]
    span = rows + block_rows
    outs = []
    for block in range(rows // block_rows):
        low = block * block_rows
        query = queries[:, low : low + block_rows]
        keys = key_cat[low : low + span]
        values = value_cat[low : low + span]
        position = low + jnp.arange(span, dtype=jnp.int32)
        own = rows + low + jnp.arange(block_rows, dtype=jnp.int32)
        allowed = (position[None, :] >= first_key[low : low + block_rows, None]) & (
            position[None, :] <= own[:, None]
        )
        scores = jnp.einsum("hqd,kd->hqk", query, keys, preferred_element_type=jnp.float32)
        scores = jnp.where(allowed[None], scores * 0.125, -1e30)
        exponent = jnp.exp(scores - jnp.max(scores, axis=-1, keepdims=True))
        weights = (exponent / jnp.sum(exponent, axis=-1, keepdims=True)).astype(jnp.bfloat16)
        result = jnp.einsum("hqk,kd->qhd", weights, values, preferred_element_type=jnp.float32)
        outs.append(result.astype(jnp.bfloat16).reshape(block_rows, -1))
    return jnp.concatenate(outs, axis=0)


def body(
    tokens,
    attn_gain,
    ffn_gain,
    w_query,
    key_value_weight,
    w_out,
    segment_ids,
    expert_ids,
    route_weights,
    w_gate,
    w_up,
    w_down,
    page_table,
):
    y, zl, zh, x, c = (lax.axis_index(name) for name in AXES)
    width = tokens.shape[1]
    tok = tokens.shape[0]
    rows = 8 * tok
    own_pack = jnp.concatenate([w_query.T, key_value_weight.T, w_out], axis=0)
    part = own_pack.shape[0] // 4
    far_part = swap_half(lax.dynamic_slice_in_dim(own_pack, y * part, part, 0))
    far_pack = in_order(from_all(far_part, ahead_y), y).reshape(-1, width)
    own_cols, far_cols = (own_pack[:128], far_pack[:128])
    other_own = swap_core(own_cols)
    other_far = swap_core(far_cols)
    normed_in = rms_scale(tokens, attn_gain)
    near = from_all(normed_in, ahead_x).reshape(4 * tok, width)

    def project(cols):
        return lax.dot_general(
            near, cols, (((1,), (1,)), ((), ())), preferred_element_type=jnp.float32
        ).astype(jnp.bfloat16)

    keep = jnp.concatenate([project(own_cols), project(far_cols)], axis=1)
    give = jnp.concatenate([project(other_own), project(other_far)], axis=1)
    got = swap_core(give)
    both = jnp.where(c == 0, jnp.stack([keep, got]), jnp.stack([got, keep]))
    both = both.reshape(2, 4, tok, 256).transpose(1, 0, 2, 3)
    projected = in_order(both, x).reshape(rows, 256)
    queries = jnp.stack([projected[:, 0:64], projected[:, 128:192]])
    own_kv, far_kv = (projected[:, 64:128], projected[:, 192:256])
    key_rows = jnp.where(zh == 0, own_kv, far_kv)
    value_rows = jnp.where(zh == 0, far_kv, own_kv)
    key_value = jnp.concatenate([key_rows, value_rows], axis=1)
    partner = swap_half(key_value)
    shifted = next_group(partner)
    before = jnp.where(zh == 0, shifted, partner)
    seg_near = from_all(segment_ids, ahead_x)
    seg_got = swap_core(seg_near)
    seg = jnp.where(c == 0, jnp.stack([seg_near, seg_got]), jnp.stack([seg_got, seg_near]))
    seg = in_order(seg.transpose(1, 0, 2), x).reshape(rows)
    base = ((y * 8 + zl) * 2 + zh) * rows
    first_key = seg - base + rows
    key_cat = jnp.concatenate([before[:, :64], key_rows], axis=0)
    value_cat = jnp.concatenate([before[:, 64:], value_rows], axis=0)
    attended = attend(queries, key_cat, value_cat, first_key, 512)
    group_kv = jnp.where(zh == 0, jnp.stack([key_value, partner]), jnp.stack([partner, key_value]))
    page_order = page_table[0]
    page_ids = zh * 64 + jnp.arange(64, dtype=jnp.int32)
    block_ids = jnp.arange(128, dtype=jnp.int32)
    source_block = jnp.sum(
        jnp.where(page_order[None, :] == page_ids[:, None], block_ids[None, :], 0), axis=1
    )
    pages = group_kv.reshape(128, PAGE, 128)[source_block]
    joined = jnp.concatenate([attended.reshape(8, tok, 128), pages.reshape(8, tok, 128)], axis=1)
    joined = lax.all_to_all(joined, ROW, split_axis=0, concat_axis=0, tiled=True)
    token_heads = joined[:, :tok].transpose(1, 0, 2).reshape(tok, 1024)
    kv_cache = joined[:, tok:].reshape(8, 8, PAGE, 2, 64).transpose(1, 2, 3, 0, 4)
    kv_cache = kv_cache.reshape(8, PAGE, 1024)
    out_rows = jnp.concatenate([own_pack[128:], far_pack[128:]], axis=0)
    out_all = lax.all_gather(out_rows, ROW, axis=0, tiled=True)
    out_sum = jnp.dot(token_heads, out_all, preferred_element_type=jnp.float32)
    mid_state = (tokens.astype(jnp.float32) + out_sum).astype(jnp.bfloat16)
    normed_mid = rms_scale(mid_state, ffn_gain)
    gate_up = jnp.concatenate([w_gate, w_up], axis=1)
    piece = y * 2 + zl % 2

    def far_weight(own):
        step = own.shape[0] // 8
        eighth = swap_half(lax.dynamic_slice_in_dim(own, piece * step, step, 0))
        beside = swap_near(eighth)
        pair = jnp.where(
            zl % 2 == 0,
            jnp.concatenate([eighth, beside], axis=0),
            jnp.concatenate([beside, eighth], axis=0),
        )
        return lax.all_gather(pair, "y", axis=0, tiled=True)

    def whole(own):
        far = far_weight(own)
        mine = c == zh
        kept = jnp.where(mine, own, far)
        return (kept, swap_core(jnp.where(mine, far, own)))

    gate_up_a, gate_up_b = whole(gate_up)
    down_a, down_b = whole(w_down)
    flat = expert_ids.reshape(-1)
    onehot = (flat[:, None] == jnp.arange(8, dtype=jnp.int32)[None, :]).astype(jnp.int32)
    earlier = jnp.cumsum(onehot, axis=0) - onehot
    slot = jnp.sum(earlier * onehot, axis=-1)
    holder = flat % 4 * 2 + flat // 4
    target_slot = (holder * CAP + slot).reshape(tok, 2)
    slots = jnp.arange(8 * CAP, dtype=jnp.int32)
    pick = [(target_slot[:, k : k + 1] == slots[None, :]).astype(jnp.bfloat16) for k in range(2)]
    send = lax.dot_general(
        pick[0] + pick[1], normed_mid, (((0,), (0,)), ((), ())), preferred_element_type=jnp.float32
    ).astype(jnp.bfloat16)
    arrived = lax.all_to_all(
        send.reshape(8, CAP, width), ROW, split_axis=0, concat_axis=0, tiled=True
    ).reshape(8 * CAP, width)

    def half(gate_up_half, down_half):
        both_act = jnp.dot(arrived, gate_up_half, preferred_element_type=jnp.float32)
        gate_act, up_act = (both_act[:, :256], both_act[:, 256:])
        activated = (jax.nn.silu(gate_act) * up_act).astype(jnp.bfloat16)
        return jnp.dot(activated, down_half, preferred_element_type=jnp.float32)

    expert_out = (half(gate_up_a, down_a) + half(gate_up_b, down_b)).astype(jnp.bfloat16)
    returned = lax.all_to_all(
        expert_out.reshape(8, CAP, width), ROW, split_axis=0, concat_axis=0, tiled=True
    ).reshape(8 * CAP, width)
    total = mid_state.astype(jnp.float32)
    for k in range(2):
        chosen = jnp.dot(pick[k], returned, preferred_element_type=jnp.float32)
        total = total + chosen * route_weights[:, k : k + 1]
    return (total.astype(jnp.bfloat16), kv_cache)


def solution(mesh):
    fine = Mesh(mesh.devices.reshape(SIZES), AXES)
    grp, tp = (("y", "zl"), ("zh", "x", "c"))
    in_specs = (
        P(AXES, None),
        P(),
        P(),
        P(None, tp),
        P(None, tp),
        P(tp, None),
        P(AXES),
        P(AXES, None),
        P(AXES, None),
        P(None, tp),
        P(None, tp),
        P(tp, None),
        P(grp, None),
    )
    out_specs = (P(AXES, None), P(AXES, None, None))
    return jax.shard_map(body, mesh=fine, in_specs=in_specs, out_specs=out_specs, check_vma=False)
```

profile of v0, /device:TPU:40, one launch (start us, length us, event | category | flops | bytes accessed | tf_op | source)
XLA Modules:
  0.0 277.2 jit_solution(10554161021707727774)
XLA Ops:
  10.4 4.7 %collective-permute-start = (bf16[128,1536]{1,0:T(8,128)(2,1)}, bf16[128,1536]{1,0:T(8,128)(2,1)}, u32[]{:S(2)}, u32[]{:S(2)}) collective-permute-start(bf16[128,1536]{1,0:T(8,128)(2,1)} %fusion.30), channel_id=1, source_target_pairs={{0,6},{1,7},{2,0},{3,1},{4,2},{5,3},{6,4},{7,5},{8,14},{9,15},{10,... | collective-permute-start | bytes 1179656 | tf_op jit(solution)/shard_map/ppermute | solution.py:23
  15.1 2.7 collective-permute-start.1
  17.8 3.1 %collective-permute-start.12 = (s32[128]{0:T(128)}, s32[128]{0:T(128)S(1)}, u32[]{:S(2)}, u32[]{:S(2)}) collective-permute-start(s32[128]{0:T(128)} %param.19), channel_id=1, source_target_pairs={{0,6},{1,7},{2,0},{3,1},{4,2},{5,3},{6,4},{7,5},{8,14},{9,15},{10,... | collective-permute-start | bytes 1544 | tf_op jit(solution)/shard_map/ppermute | solution.py:23
  20.9 3.7 %collective-permute-start.13 = (s32[128]{0:T(128)}, s32[128]{0:T(128)S(1)}, u32[]{:S(2)}, u32[]{:S(2)}) collective-permute-start(s32[128]{0:T(128)} %param.19), channel_id=1, source_target_pairs={{0,4},{1,5},{2,6},{3,7},{4,0},{5,1},{6,2},{7,3},{8,12},{9,13},{10,... | collective-permute-start | bytes 1544 | tf_op jit(solution)/shard_map/ppermute | solution.py:23
  24.6 3.1 %collective-permute-start.14 = (s32[128]{0:T(128)}, s32[128]{0:T(128)S(1)}, u32[]{:S(2)}, u32[]{:S(2)}) collective-permute-start(s32[128]{0:T(128)} %param.19), channel_id=1, source_target_pairs={{0,2},{1,3},{2,4},{3,5},{4,6},{5,7},{6,0},{7,1},{8,10},{9,11},{10,... | collective-permute-start | bytes 1544 | tf_op jit(solution)/shard_map/ppermute | solution.py:23
  34.4 2.4 collective-permute-start.2
  36.8 14.8 %collective-permute-start.3 = (bf16[48,1536]{1,0:T(8,128)(2,1)S(1)}, bf16[48,1536]{1,0:T(8,128)(2,1)S(1)}, u32[]{:S(2)}, u32[]{:S(2)}) collective-permute-start(bf16[48,1536]{1,0:T(8,128)(2,1)S(1)} %fusion.56), channel_id=1, source_target_pairs={{0,8},{1,9},{2,10},{3,11},{4,12},{5,13},{6,14},{7,15},{8,0},{9,1},... | collective-permute-start | bytes 442376 | tf_op jit(solution)/shard_map/ppermute | solution.py:23
  56.7 13.9 %collective-permute-done.3 = bf16[48,1536]{1,0:T(8,128)(2,1)S(1)} collective-permute-done((bf16[48,1536]{1,0:T(8,128)(2,1)S(1)}, bf16[48,1536]{1,0:T(8,128)(2,1)S(1)}, u32[]{:S(2)}, u32[]{:S(2)}) %collective-permute-start.3) | collective-permute-done | bytes 147488 | tf_op jit(solution)/shard_map/ppermute | solution.py:23
  70.6 2.3 collective-permute-start.4
  73.6 4.0 %collective-permute-done.4 = bf16[48,1536]{1,0:T(8,128)(2,1)S(1)} collective-permute-done((bf16[48,1536]{1,0:T(8,128)(2,1)S(1)}, bf16[48,1536]{1,0:T(8,128)(2,1)S(1)}, u32[]{:S(2)}, u32[]{:S(2)}) %collective-permute-start.4) | collective-permute-done | bytes 147488 | tf_op jit(solution)/shard_map/ppermute | solution.py:23
  77.6 5.4 %collective-permute-start.5 = (bf16[48,1536]{1,0:T(8,128)(2,1)S(1)}, bf16[48,1536]{1,0:T(8,128)(2,1)S(1)}, u32[]{:S(2)}, u32[]{:S(2)}) collective-permute-start(bf16[48,1536]{1,0:T(8,128)(2,1)S(1)} %collective-permute-done.3), channel_id=1, source_target_pairs={{0,256},{1,257},{2,258},{3,259},{4,260},{5,261},{6,262},{7,263},{8... | collective-permute-start | bytes 442376 | tf_op jit(solution)/shard_map/ppermute | solution.py:23
  85.6 3.5 %collective-permute-start.6 = (bf16[48,1536]{1,0:T(8,128)(2,1)S(1)}, bf16[48,1536]{1,0:T(8,128)(2,1)S(1)}, u32[]{:S(2)}, u32[]{:S(2)}) collective-permute-start(bf16[48,1536]{1,0:T(8,128)(2,1)S(1)} %collective-permute-done.3), channel_id=1, source_target_pairs={{0,128},{1,129},{2,130},{3,131},{4,132},{5,133},{6,134},{7,135},{8... | collective-permute-start | bytes 442376 | tf_op jit(solution)/shard_map/ppermute | solution.py:23
  91.7 5.7 %collective-permute-done.17 = bf16[192,512]{1,0:T(8,128)(2,1)S(1)} collective-permute-done((bf16[192,512]{1,0:T(8,128)(2,1)S(1)}, bf16[192,512]{1,0:T(8,128)(2,1)S(1)}, u32[]{:S(2)}, u32[]{:S(2)}) %collective-permute-start.17) | collective-permute-done | bytes 196640 | tf_op jit(solution)/shard_map/ppermute | solution.py:23
  100.3 9.6 %collective-permute-start.18 = (bf16[32,1536]{1,0:T(8,128)(2,1)}, bf16[32,1536]{1,0:T(8,128)(2,1)}, u32[]{:S(2)}, u32[]{:S(2)}) collective-permute-start(bf16[32,1536]{1,0:T(8,128)(2,1)} %constant_dynamic-slice_fusion), channel_id=1, source_target_pairs={{0,8},{1,9},{2,10},{3,11},{4,12},{5,13},{6,14},{7,15},{8,0},{9,1},... | collective-permute-start | bytes 294920 | tf_op jit(solution)/shard_map/ppermute | solution.py:23
  122.5 2.2 collective-permute-start.9
  130.0 5.0 %collective-permute-start.10 = (bf16[1024,128]{0,1:T(8,128)(2,1)S(1)}, bf16[1024,128]{0,1:T(8,128)(2,1)S(1)}, u32[]{:S(2)}, u32[]{:S(2)}) collective-permute-start(bf16[1024,128]{0,1:T(8,128)(2,1)S(1)} %get-tuple-element.13), channel_id=1, source_target_pairs={{0,8},{1,9},{2,10},{3,11},{4,12},{5,13},{6,14},{7,15},{8,0},{9,1},... | collective-permute-start | bytes 786440 | tf_op jit(solution)/shard_map/ppermute | solution.py:23
  136.6 25.3 %collective-permute-done.10 = bf16[1024,128]{0,1:T(8,128)(2,1)S(1)} collective-permute-done((bf16[1024,128]{0,1:T(8,128)(2,1)S(1)}, bf16[1024,128]{0,1:T(8,128)(2,1)S(1)}, u32[]{:S(2)}, u32[]{:S(2)}) %collective-permute-start.10) | collective-permute-done | bytes 262176 | tf_op jit(solution)/shard_map/ppermute | solution.py:23
  166.8 5.3 %collective-permute-done.11 = bf16[1024,128]{0,1:T(8,128)(2,1)} collective-permute-done((bf16[1024,128]{0,1:T(8,128)(2,1)S(1)}, bf16[1024,128]{0,1:T(8,128)(2,1)}, u32[]{:S(2)}, u32[]{:S(2)}) %collective-permute-start.11) | collective-permute-done | bytes 262176 | tf_op jit(solution)/shard_map/ppermute | solution.py:23
  173.8 3.3 %fusion.126 = f32[2,512]{1,0:T(2,128)S(1)} fusion(pred[512,1536]{1,0:T(8,128)(4,1)S(1)} %copy-done.6, bf16[1024,64]{0,1:T(8,128)(2,1)S(1)} %get-tuple-element.11, bf16[1024,64]{0,1:T(8,128)(2,1)} %copy-done.10, bf16[1,1024,64]{1,2,0:T(8,128)(2,1)} %get-tuple-element.6, bf16[1,1024,64]{1,2,0:T(8,128)(2,1)} %get-tuple-element.7), kind=kOutput, calls=%fused_computation.196 | convolution fusion | flops 208078336 | bytes 1314816 | tf_op jit(solution)/shard_map/sub | solution.py:87
  177.1 4.7 %fusion.23 = bf16[64,2,512]{2,0,1:T(8,128)(2,1)} fusion(f32[2,512]{1,0:T(2,128)S(1)} %fusion.126, pred[512,1536]{1,0:T(8,128)(4,1)S(1)} %copy-done.6, bf16[1024,64]{0,1:T(8,128)(2,1)} %get-tuple-element.10, bf16[1024,64]{0,1:T(8,128)(2,1)} %copy-done.12, bf16[1024,64]{0,1:T(8,128)(2,1)} %copy-done.15, bf16[1024,64]{0,1:T(8,128)(2,1)} %copy-done.10, ...), kind=kOutput, calls=%fused_computation.42 | convolution fusion | flops 411437568 | bytes 1708032 | tf_op jit(solution)/shard_map/hqk,kd->qhd/dot_general | solution.py:89
  181.8 3.4 %fusion.123 = f32[2,512]{1,0:T(2,128)S(1)} fusion(pred[512,1536]{1,0:T(8,128)(4,1)S(1)} %copy-done.5, bf16[1024,64]{0,1:T(8,128)(2,1)} %copy-done.10, bf16[1024,64]{0,1:T(8,128)(2,1)} %copy-done.15, bf16[1,1024,64]{1,2,0:T(8,128)(2,1)} %get-tuple-element.7, bf16[1,1024,64]{1,2,0:T(8,128)(2,1)} %get-tuple-element.6), kind=kOutput, calls=%fused_computation.195 | convolution fusion | flops 208274944 | bytes 1314816 | tf_op jit(solution)/shard_map/sub | solution.py:87
  185.2 3.8 %fusion.22 = bf16[64,2,512]{2,0,1:T(8,128)(2,1)S(1)} fusion(f32[2,512]{1,0:T(2,128)S(1)} %fusion.123, pred[512,1536]{1,0:T(8,128)(4,1)S(1)} %copy-done.5, bf16[1024,64]{0,1:T(8,128)(2,1)S(1)} %copy-done.13, bf16[1024,64]{0,1:T(8,128)(2,1)S(1)} %copy-done.14, bf16[1024,64]{0,1:T(8,128)(2,1)S(1)} %copy-done.11, bf16[1024,64]{0,1:T(8,128)(2,1)S(1)} %copy-done.16, ...), kind=kOutput, calls=%fused_computation.41 | convolution fusion | flops 411634176 | bytes 1708032 | tf_op jit(solution)/shard_map/hqk,kd->qhd/dot_general | solution.py:89
  190.0 4.4 %all-to-all-start = ((bf16[8,256,128]{2,1,0:T(8,128)(2,1)}), bf16[8,256,128]{2,1,0:T(8,128)(2,1)S(1)}, u32[]{:S(2)}, u32[]{:S(2)}) async-start(bf16[8,256,128]{2,1,0:T(8,128)(2,1)} %pad_maximum_fusion.1), calls=%async_computation | async-start | bytes 1048576 | tf_op jit(solution)/shard_map/all_to_all | solution.py:160
  197.0 7.8 %all-to-all-done = bf16[8,256,128]{2,1,0:T(8,128)(2,1)S(1)} async-done(((bf16[8,256,128]{2,1,0:T(8,128)(2,1)}), bf16[8,256,128]{2,1,0:T(8,128)(2,1)S(1)}, u32[]{:S(2)}, u32[]{:S(2)}) %all-to-all-start) | async-done | bytes 524320 | tf_op jit(solution)/shard_map/all_to_all | solution.py:160
  205.1 2.8 broadcast_select_fusion
  209.8 2.6 multiply_reduce_fusion
  214.0 4.3 %all-to-all-start.1 = ((bf16[8,48,1536]{2,1,0:T(8,128)(2,1)}), bf16[8,48,1536]{2,1,0:T(8,128)(2,1)}, u32[]{:S(2)}, u32[]{:S(2)}) async-start(bf16[8,48,1536]{2,1,0:T(8,128)(2,1)} %bitcast.44), calls=%async_computation.1 | async-start | bytes 2359296 | tf_op jit(solution)/shard_map/all_to_all | solution.py:202
  219.4 16.0 %all_gather.11 = bf16[256,1536]{1,0:T(8,128)(2,1)S(1)} all-gather(bf16[64,1536]{1,0:T(8,128)(2,1)S(1)} %maximum_select_fusion.3), channel_id=1, replica_groups=mesh['y'=4,'zl'=8,'zh'=2,'x'=4,'c'=2] {'y'}, dimensions={0}, use_global_device_ids=true | all-gather | bytes 983040 | tf_op jit(solution)/shard_map/all_gather | solution.py:181
  238.4 2.6 fusion.131
  243.7 2.7 fusion.13
  246.4 4.9 %all-to-all-start.2 = ((bf16[8,48,1536]{2,1,0:T(8,128)(2,1)}), bf16[8,48,1536]{2,1,0:T(8,128)(2,1)S(1)}, u32[]{:S(2)}, u32[]{:S(2)}) async-start(bf16[8,48,1536]{2,1,0:T(8,128)(2,1)} %bitcast.46), calls=%async_computation.2 | async-start | bytes 2359296 | tf_op jit(solution)/shard_map/all_to_all | solution.py:213
  253.3 15.4 %all-to-all-done.2 = bf16[8,48,1536]{2,1,0:T(8,128)(2,1)S(1)} async-done(((bf16[8,48,1536]{2,1,0:T(8,128)(2,1)}), bf16[8,48,1536]{2,1,0:T(8,128)(2,1)S(1)}, u32[]{:S(2)}, u32[]{:S(2)}) %all-to-all-start.2) | async-done | bytes 1179680 | tf_op jit(solution)/shard_map/all_to_all | solution.py:213
  (168 shorter events, 66.7 us)
Async XLA Ops:
  7.2 21.8 %copy-start.19 = (s32[128,2]{0,1:T(2,128)S(1)}, s32[128,2]{0,1:T(2,128)}, u32[]{:S(2)}) copy-start(s32[128,2]{0,1:T(2,128)} %param.20) | copy-start | bytes 3076
  7.2 22.2 %copy-start.22 = (s32[1,128]{1,0:T(1,128)S(1)}, s32[1,128]{1,0:T(1,128)}, u32[]{:S(2)}) copy-start(s32[1,128]{1,0:T(1,128)} %param.25) | copy-start | bytes 1540
  7.2 23.3 %copy-start.4 = (bf16[1536,256]{1,0:T(8,128)(2,1)S(1)}, bf16[1536,256]{1,0:T(8,128)(2,1)}, u32[]{:S(2)}) copy-start(bf16[1536,256]{1,0:T(8,128)(2,1)} %param.22) | copy-start | bytes 2359300
  7.2 197.9 %all-gather.5.cloned.1.call-start = ((), (), s32[]{:S(2)}) async-start(), calls=%async_computation.4 | async-start | bytes 1966080 | tf_op jit(solution)/shard_map/all_gather | solution.py:181
  8.5 22.1 %copy-start.8 = (bf16[1536,64]{0,1:T(8,128)(2,1)S(1)}, bf16[1536,64]{0,1:T(8,128)(2,1)}, u32[]{:S(2)}) copy-start(bf16[1536,64]{0,1:T(8,128)(2,1)} %param.16) | copy-start | bytes 589828
  8.5 22.1 %copy-start.9 = (bf16[1536,64]{0,1:T(8,128)(2,1)S(1)}, bf16[1536,64]{0,1:T(8,128)(2,1)}, u32[]{:S(2)}) copy-start(bf16[1536,64]{0,1:T(8,128)(2,1)} %param.17) | copy-start | bytes 589828
  10.4 105.5 %collective-permute-start = (bf16[128,1536]{1,0:T(8,128)(2,1)}, bf16[128,1536]{1,0:T(8,128)(2,1)}, u32[]{:S(2)}, u32[]{:S(2)}) collective-permute-start(bf16[128,1536]{1,0:T(8,128)(2,1)} %fusion.30), channel_id=1, source_target_pairs={{0,6},{1,7},{2,0},{3,1},{4,2},{5,3},{6,4},{7,5},{8,14},{9,15},{10,... | collective-permute-start | bytes 1179656 | tf_op jit(solution)/shard_map/ppermute | solution.py:23
  15.1 103.0 %collective-permute-start.1 = (bf16[128,1536]{1,0:T(8,128)(2,1)}, bf16[128,1536]{1,0:T(8,128)(2,1)}, u32[]{:S(2)}, u32[]{:S(2)}) collective-permute-start(bf16[128,1536]{1,0:T(8,128)(2,1)} %fusion.30), channel_id=1, source_target_pairs={{0,4},{1,5},{2,6},{3,7},{4,0},{5,1},{6,2},{7,3},{8,12},{9,13},{10,... | collective-permute-start | bytes 1179656 | tf_op jit(solution)/shard_map/ppermute | solution.py:23
  17.8 16.5 %collective-permute-start.12 = (s32[128]{0:T(128)}, s32[128]{0:T(128)S(1)}, u32[]{:S(2)}, u32[]{:S(2)}) collective-permute-start(s32[128]{0:T(128)} %param.19), channel_id=1, source_target_pairs={{0,6},{1,7},{2,0},{3,1},{4,2},{5,3},{6,4},{7,5},{8,14},{9,15},{10,... | collective-permute-start | bytes 1544 | tf_op jit(solution)/shard_map/ppermute | solution.py:23
  20.9 15.9 %collective-permute-start.13 = (s32[128]{0:T(128)}, s32[128]{0:T(128)S(1)}, u32[]{:S(2)}, u32[]{:S(2)}) collective-permute-start(s32[128]{0:T(128)} %param.19), channel_id=1, source_target_pairs={{0,4},{1,5},{2,6},{3,7},{4,0},{5,1},{6,2},{7,3},{8,12},{9,13},{10,... | collective-permute-start | bytes 1544 | tf_op jit(solution)/shard_map/ppermute | solution.py:23
  24.6 27.0 %collective-permute-start.14 = (s32[128]{0:T(128)}, s32[128]{0:T(128)S(1)}, u32[]{:S(2)}, u32[]{:S(2)}) collective-permute-start(s32[128]{0:T(128)} %param.19), channel_id=1, source_target_pairs={{0,2},{1,3},{2,4},{3,5},{4,6},{5,7},{6,0},{7,1},{8,10},{9,11},{10,... | collective-permute-start | bytes 1544 | tf_op jit(solution)/shard_map/ppermute | solution.py:23
  34.4 83.8 %collective-permute-start.2 = (bf16[128,1536]{1,0:T(8,128)(2,1)}, bf16[128,1536]{1,0:T(8,128)(2,1)}, u32[]{:S(2)}, u32[]{:S(2)}) collective-permute-start(bf16[128,1536]{1,0:T(8,128)(2,1)} %fusion.30), channel_id=1, source_target_pairs={{0,2},{1,3},{2,4},{3,5},{4,6},{5,7},{6,0},{7,1},{8,10},{9,11},{10,... | collective-permute-start | bytes 1179656 | tf_op jit(solution)/shard_map/ppermute | solution.py:23
  36.8 33.8 %collective-permute-start.3 = (bf16[48,1536]{1,0:T(8,128)(2,1)S(1)}, bf16[48,1536]{1,0:T(8,128)(2,1)S(1)}, u32[]{:S(2)}, u32[]{:S(2)}) collective-permute-start(bf16[48,1536]{1,0:T(8,128)(2,1)S(1)} %fusion.56), channel_id=1, source_target_pairs={{0,8},{1,9},{2,10},{3,11},{4,12},{5,13},{6,14},{7,15},{8,0},{9,1},... | collective-permute-start | bytes 442376 | tf_op jit(solution)/shard_map/ppermute | solution.py:23
  51.6 3.1 %collective-permute-start.15 = (s32[4,128]{1,0:T(4,128)S(1)}, s32[4,128]{1,0:T(4,128)S(1)}, u32[]{:S(2)}, u32[]{:S(2)}) collective-permute-start(s32[4,128]{1,0:T(4,128)S(1)} %get-tuple-element.17), channel_id=1, source_target_pairs={{0,1},{1,0},{2,3},{3,2},{4,5},{5,4},{6,7},{7,6},{8,9},{9,8},{10,11... | collective-permute-start | bytes 6152 | tf_op jit(solution)/shard_map/ppermute | solution.py:23
  54.7 30.9 %collective-permute-start.16 = (bf16[192,512]{1,0:T(8,128)(2,1)S(1)}, bf16[192,512]{1,0:T(8,128)(2,1)S(1)}, u32[]{:S(2)}, u32[]{:S(2)}) collective-permute-start(bf16[192,512]{1,0:T(8,128)(2,1)S(1)} %constant_dynamic-slice_fusion.1), channel_id=1, source_target_pairs={{0,8},{1,9},{2,10},{3,11},{4,12},{5,13},{6,14},{7,15},{8,0},{9,1},... | collective-permute-start | bytes 589832 | tf_op jit(solution)/shard_map/ppermute | solution.py:23
  70.6 7.0 %collective-permute-start.4 = (bf16[48,1536]{1,0:T(8,128)(2,1)S(1)}, bf16[48,1536]{1,0:T(8,128)(2,1)S(1)}, u32[]{:S(2)}, u32[]{:S(2)}) collective-permute-start(bf16[48,1536]{1,0:T(8,128)(2,1)S(1)} %collective-permute-done.3), channel_id=1, source_target_pairs={{0,384},{1,385},{2,386},{3,387},{4,388},{5,389},{6,390},{7,391},{8... | collective-permute-start | bytes 442376 | tf_op jit(solution)/shard_map/ppermute | solution.py:23
  77.6 11.4 %collective-permute-start.5 = (bf16[48,1536]{1,0:T(8,128)(2,1)S(1)}, bf16[48,1536]{1,0:T(8,128)(2,1)S(1)}, u32[]{:S(2)}, u32[]{:S(2)}) collective-permute-start(bf16[48,1536]{1,0:T(8,128)(2,1)S(1)} %collective-permute-done.3), channel_id=1, source_target_pairs={{0,256},{1,257},{2,258},{3,259},{4,260},{5,261},{6,262},{7,263},{8... | collective-permute-start | bytes 442376 | tf_op jit(solution)/shard_map/ppermute | solution.py:23
  85.6 14.7 %collective-permute-start.6 = (bf16[48,1536]{1,0:T(8,128)(2,1)S(1)}, bf16[48,1536]{1,0:T(8,128)(2,1)S(1)}, u32[]{:S(2)}, u32[]{:S(2)}) collective-permute-start(bf16[48,1536]{1,0:T(8,128)(2,1)S(1)} %collective-permute-done.3), channel_id=1, source_target_pairs={{0,128},{1,129},{2,130},{3,131},{4,132},{5,133},{6,134},{7,135},{8... | collective-permute-start | bytes 442376 | tf_op jit(solution)/shard_map/ppermute | solution.py:23
  89.1 8.3 %collective-permute-start.17 = (bf16[192,512]{1,0:T(8,128)(2,1)S(1)}, bf16[192,512]{1,0:T(8,128)(2,1)S(1)}, u32[]{:S(2)}, u32[]{:S(2)}) collective-permute-start(bf16[192,512]{1,0:T(8,128)(2,1)S(1)} %collective-permute-done.16), channel_id=1, source_target_pairs={{0,16},{1,17},{2,18},{3,19},{4,20},{5,21},{6,22},{7,23},{8,24},{9,... | collective-permute-start | bytes 589832 | tf_op jit(solution)/shard_map/ppermute | solution.py:23
  97.4 22.8 %collective-permute-start.7 = (bf16[128,1536]{1,0:T(8,128)(2,1)}, bf16[128,1536]{1,0:T(8,128)(2,1)}, u32[]{:S(2)}, u32[]{:S(2)}) collective-permute-start(bf16[128,1536]{1,0:T(8,128)(2,1)} %pad_maximum_fusion.2), channel_id=1, source_target_pairs={{0,1},{1,0},{2,3},{3,2},{4,5},{5,4},{6,7},{7,6},{8,9},{9,8},{10,11... | collective-permute-start | bytes 1179656 | tf_op jit(solution)/shard_map/ppermute | solution.py:23
  100.2 109.6 %all-gather.3.cloned.1.call-start = ((), (), s32[]{:S(2)}) async-start(), calls=%async_computation.3 | async-start | bytes 3538944 | tf_op jit(solution)/shard_map/all_gather | solution.py:165
  100.3 94.6 %collective-permute-start.18 = (bf16[32,1536]{1,0:T(8,128)(2,1)}, bf16[32,1536]{1,0:T(8,128)(2,1)}, u32[]{:S(2)}, u32[]{:S(2)}) collective-permute-start(bf16[32,1536]{1,0:T(8,128)(2,1)} %constant_dynamic-slice_fusion), channel_id=1, source_target_pairs={{0,8},{1,9},{2,10},{3,11},{4,12},{5,13},{6,14},{7,15},{8,0},{9,1},... | collective-permute-start | bytes 294920 | tf_op jit(solution)/shard_map/ppermute | solution.py:23
  116.0 5.9 %collective-permute-start.8 = (bf16[128,1536]{1,0:T(8,128)(2,1)}, bf16[128,1536]{1,0:T(8,128)(2,1)S(1)}, u32[]{:S(2)}, u32[]{:S(2)}) collective-permute-start(bf16[128,1536]{1,0:T(8,128)(2,1)} %slice.124), channel_id=1, source_target_pairs={{0,1},{1,0},{2,3},{3,2},{4,5},{5,4},{6,7},{7,6},{8,9},{9,8},{10,11... | collective-permute-start | bytes 1179656 | tf_op jit(solution)/shard_map/ppermute | solution.py:23
  122.5 3.4 %collective-permute-start.9 = (bf16[512,256]{0,1:T(8,128)(2,1)S(1)}, bf16[512,256]{0,1:T(8,128)(2,1)S(1)}, u32[]{:S(2)}, u32[]{:S(2)}) collective-permute-start(bf16[512,256]{0,1:T(8,128)(2,1)S(1)} %pad_maximum_fusion.5), channel_id=1, source_target_pairs={{0,1},{1,0},{2,3},{3,2},{4,5},{5,4},{6,7},{7,6},{8,9},{9,8},{10,11... | collective-permute-start | bytes 786440 | tf_op jit(solution)/shard_map/ppermute | solution.py:23
  130.0 31.8 %collective-permute-start.10 = (bf16[1024,128]{0,1:T(8,128)(2,1)S(1)}, bf16[1024,128]{0,1:T(8,128)(2,1)S(1)}, u32[]{:S(2)}, u32[]{:S(2)}) collective-permute-start(bf16[1024,128]{0,1:T(8,128)(2,1)S(1)} %get-tuple-element.13), channel_id=1, source_target_pairs={{0,8},{1,9},{2,10},{3,11},{4,12},{5,13},{6,14},{7,15},{8,0},{9,1},... | collective-permute-start | bytes 786440 | tf_op jit(solution)/shard_map/ppermute | solution.py:23
  161.9 10.3 %collective-permute-start.11 = (bf16[1024,128]{0,1:T(8,128)(2,1)S(1)}, bf16[1024,128]{0,1:T(8,128)(2,1)}, u32[]{:S(2)}, u32[]{:S(2)}) collective-permute-start(bf16[1024,128]{0,1:T(8,128)(2,1)S(1)} %collective-permute-done.10), channel_id=1, source_target_pairs={{0,16},{1,17},{2,18},{3,19},{4,20},{5,21},{6,22},{7,23},{16,32},{1... | collective-permute-start | bytes 786440 | tf_op jit(solution)/shard_map/ppermute | solution.py:23
  190.0 14.8 %all-to-all-start = ((bf16[8,256,128]{2,1,0:T(8,128)(2,1)}), bf16[8,256,128]{2,1,0:T(8,128)(2,1)S(1)}, u32[]{:S(2)}, u32[]{:S(2)}) async-start(bf16[8,256,128]{2,1,0:T(8,128)(2,1)} %pad_maximum_fusion.1), calls=%async_computation | async-start | bytes 1048576 | tf_op jit(solution)/shard_map/all_to_all | solution.py:160
  194.9 23.4 %collective-permute-start.19 = (bf16[32,1536]{1,0:T(8,128)(2,1)}, bf16[32,1536]{1,0:T(8,128)(2,1)S(1)}, u32[]{:S(2)}, u32[]{:S(2)}) collective-permute-start(bf16[32,1536]{1,0:T(8,128)(2,1)} %collective-permute-done.18), channel_id=1, source_target_pairs={{0,16},{1,17},{2,18},{3,19},{4,20},{5,21},{6,22},{7,23},{8,24},{9,... | collective-permute-start | bytes 294920 | tf_op jit(solution)/shard_map/ppermute | solution.py:23
  207.9 30.5 %collective-permute-start.20 = (bf16[1536,512]{1,0:T(8,128)(2,1)}, bf16[1536,512]{1,0:T(8,128)(2,1)}, u32[]{:S(2)}, u32[]{:S(2)}) collective-permute-start(bf16[1536,512]{1,0:T(8,128)(2,1)} %broadcast_select_fusion), channel_id=1, source_target_pairs={{0,1},{1,0},{2,3},{3,2},{4,5},{5,4},{6,7},{7,6},{8,9},{9,8},{10,11... | collective-permute-start | bytes 4718600 | tf_op jit(solution)/shard_map/ppermute | solution.py:23
  214.0 24.3 %all-to-all-start.1 = ((bf16[8,48,1536]{2,1,0:T(8,128)(2,1)}), bf16[8,48,1536]{2,1,0:T(8,128)(2,1)}, u32[]{:S(2)}, u32[]{:S(2)}) async-start(bf16[8,48,1536]{2,1,0:T(8,128)(2,1)} %bitcast.44), calls=%async_computation.1 | async-start | bytes 2359296 | tf_op jit(solution)/shard_map/all_to_all | solution.py:202
  236.4 7.3 %collective-permute-start.21 = (bf16[256,1536]{1,0:T(8,128)(2,1)}, bf16[256,1536]{1,0:T(8,128)(2,1)}, u32[]{:S(2)}, u32[]{:S(2)}) collective-permute-start(bf16[256,1536]{1,0:T(8,128)(2,1)} %broadcast_select_fusion.1), channel_id=1, source_target_pairs={{0,1},{1,0},{2,3},{3,2},{4,5},{5,4},{6,7},{7,6},{8,9},{9,8},{10,11... | collective-permute-start | bytes 2359304 | tf_op jit(solution)/shard_map/ppermute | solution.py:23
  246.4 22.3 %all-to-all-start.2 = ((bf16[8,48,1536]{2,1,0:T(8,128)(2,1)}), bf16[8,48,1536]{2,1,0:T(8,128)(2,1)S(1)}, u32[]{:S(2)}, u32[]{:S(2)}) async-start(bf16[8,48,1536]{2,1,0:T(8,128)(2,1)} %bitcast.46), calls=%async_computation.2 | async-start | bytes 2359296 | tf_op jit(solution)/shard_map/all_to_all | solution.py:213
  (18 other events, 92.5 us)
Sparse Core Ops, SparseCore 0:
  100.3 32.7 all-gather.4
  135.3 36.5 all-gather.2
where the time goes:
time: 279 us; the launch traced here: 277 us
  starting transfers between devices  94 us (34%)
  waiting for transfers between devices  80.8 us (29%)
  matrix products  32.4 us (12%)
  other arithmetic  21.8 us (8%)
  local copies, waits for them, and re-layouts  17 us (6%)
  blocking collectives  16 us (6%)
  between operations  15.1 us (5%)
    ppermute x22, starting transfers between devices, permute(): return lax.ppermute(block, AXES, route)  80.3 us
    ppermute x22, waiting for transfers between devices, permute(): return lax.ppermute(block, AXES, route)  57.5 us
    all_gather x1, blocking collectives, far_weight(): return lax.all_gather(pair, 'y', axis=0, tiled=True)  16 us
    all_to_all x1, waiting for transfers between devices, body(): lax.all_to_all(expert_out.reshape(8, CAP, width), ROW, split_axis=0, conc...  15.4 us
    dot_general x2, matrix products, attend(): jnp.einsum('hqk,kd->qhd', weights, values, preferred_element_type=jnp.flo...  8.46 us
    all_to_all x1, waiting for transfers between devices, body(): lax.all_to_all(joined, ROW, split_axis=0, concat_axis=0, tiled=True)  7.79 us
    sub x2, matrix products, attend(): exponent = jnp.exp(scores - jnp.max(scores, axis=-1, keepdims=True))  6.67 us
    unnamed x55, local copies, waits for them, and re-layouts  5.58 us
  transfers between devices with their start and end apart: 27, of which 10 were waited for; matrix products, arithmetic and copies ran while one was open for 23% of the time, Pallas kernels for 0%

commit v1 on v0

--- a/solution.py
+++ b/solution.py
@@ -11,6 +11,21 @@
 ROW = ("x", "c")
 PAGE = 16
 CAP = 48
+
+
+def balance_types(a0, net_axis):
+    return jnp.concatenate(
+        lax.all_to_all(
+            jnp.stack(tuple((a0 for _ in range(lax.axis_size(net_axis)))), axis=0),
+            axis_name=net_axis,
+            split_axis=0,
+            concat_axis=0,
+        ),
+        axis=0,
+    )
+
+
+launch_outputs = functools.partial(balance_types, net_axis="y")
 
 
 def permute(block, target):
@@ -178,7 +193,7 @@
             jnp.concatenate([eighth, beside], axis=0),
             jnp.concatenate([beside, eighth], axis=0),
         )
-        return lax.all_gather(pair, "y", axis=0, tiled=True)
+        return launch_outputs(pair)
 
     def whole(own):
         far = far_weight(own)

time: 279 us -> 307 us (1.10)
  the two profiles are of different devices: /device:TPU:40 before, /device:TPU:1 now
where the time goes in v1:
time: 307 us; the launch traced here: 305 us
  starting transfers between devices  129 us (42%)
  waiting for transfers between devices  81.9 us (27%)
  matrix products  31.5 us (10%)
  other arithmetic  30.6 us (10%)
  local copies, waits for them, and re-layouts  16.5 us (5%)
  between operations  15 us (5%)
    ppermute x22, starting transfers between devices, permute(): return lax.ppermute(block, AXES, route)  103 us
    ppermute x22, waiting for transfers between devices, permute(): return lax.ppermute(block, AXES, route)  48.7 us
    all_to_all x1, waiting for transfers between devices, body(): lax.all_to_all(expert_out.reshape(8, CAP, width), ROW, split_axis=0, conc...  14.6 us
    all_to_all x2, waiting for transfers between devices, balance_types(): lax.all_to_all(jnp.stack(tuple((a0 for _ in range(lax.axis_size(net_axis)...  12.4 us
    all_to_all x2, starting transfers between devices, balance_types(): lax.all_to_all(jnp.stack(tuple((a0 for _ in range(lax.axis_size(net_axis)...  11.8 us
    dot_general x2, matrix products, attend(): jnp.einsum('hqk,kd->qhd', weights, values, preferred_element_type=jnp.flo...  7.79 us
    all_to_all x1, starting transfers between devices, body(): lax.all_to_all(send.reshape(8, CAP, width), ROW, split_axis=0, concat_axi...  6.37 us
    all_to_all x1, waiting for transfers between devices, body(): lax.all_to_all(send.reshape(8, CAP, width), ROW, split_axis=0, concat_axi...  6.31 us
  transfers between devices with their start and end apart: 28, of which 11 were waited for; matrix products, arithmetic and copies ran while one was open for 23% of the time, Pallas kernels for 0%

profile of v1, /device:TPU:1, one launch (start us, length us, event | category | flops | bytes accessed | tf_op | source)
XLA Modules:
  0.0 305.0 jit_solution(3284917312257722220)
XLA Ops:
  10.4 5.2 %collective-permute-start = (bf16[128,1536]{1,0:T(8,128)(2,1)}, bf16[128,1536]{1,0:T(8,128)(2,1)}, u32[]{:S(2)}, u32[]{:S(2)}) collective-permute-start(bf16[128,1536]{1,0:T(8,128)(2,1)} %fusion.27), channel_id=1, source_target_pairs={{0,6},{1,7},{2,0},{3,1},{4,2},{5,3},{6,4},{7,5},{8,14},{9,15},{10,... | collective-permute-start | bytes 1179656 | tf_op jit(solution)/shard_map/ppermute | solution.py:38
  20.6 3.8 %collective-permute-start.13 = (s32[128]{0:T(128)}, s32[128]{0:T(128)}, u32[]{:S(2)}, u32[]{:S(2)}) collective-permute-start(s32[128]{0:T(128)} %param.19), channel_id=1, source_target_pairs={{0,4},{1,5},{2,6},{3,7},{4,0},{5,1},{6,2},{7,3},{8,12},{9,13},{10,... | collective-permute-start | bytes 1544 | tf_op jit(solution)/shard_map/ppermute | solution.py:38
  24.3 2.8 collective-permute-start.14
  40.3 15.6 %collective-permute-start.3 = (bf16[48,1536]{1,0:T(8,128)(2,1)}, bf16[48,1536]{1,0:T(8,128)(2,1)S(1)}, u32[]{:S(2)}, u32[]{:S(2)}) collective-permute-start(bf16[48,1536]{1,0:T(8,128)(2,1)} %fusion.51), channel_id=1, source_target_pairs={{0,8},{1,9},{2,10},{3,11},{4,12},{5,13},{6,14},{7,15},{8,0},{9,1},... | collective-permute-start | bytes 442376 | tf_op jit(solution)/shard_map/ppermute | solution.py:38
  56.6 4.5 %collective-permute-start.15 = (s32[4,128]{1,0:T(4,128)S(1)}, s32[4,128]{1,0:T(4,128)S(1)}, u32[]{:S(2)}, u32[]{:S(2)}) collective-permute-start(s32[4,128]{1,0:T(4,128)S(1)} %get-tuple-element.19), channel_id=1, source_target_pairs={{0,1},{1,0},{2,3},{3,2},{4,5},{5,4},{6,7},{7,6},{8,9},{9,8},{10,11... | collective-permute-start | bytes 6152 | tf_op jit(solution)/shard_map/ppermute | solution.py:38
  68.3 4.6 %collective-permute-start.4 = (bf16[48,1536]{1,0:T(8,128)(2,1)S(1)}, bf16[48,1536]{1,0:T(8,128)(2,1)S(1)}, u32[]{:S(2)}, u32[]{:S(2)}) collective-permute-start(bf16[48,1536]{1,0:T(8,128)(2,1)S(1)} %collective-permute-done.3), channel_id=1, source_target_pairs={{0,384},{1,385},{2,386},{3,387},{4,388},{5,389},{6,390},{7,391},{8... | collective-permute-start | bytes 442376 | tf_op jit(solution)/shard_map/ppermute | solution.py:38
  72.9 2.7 collective-permute-done.4
  75.6 4.3 %collective-permute-start.5 = (bf16[48,1536]{1,0:T(8,128)(2,1)S(1)}, bf16[48,1536]{1,0:T(8,128)(2,1)S(1)}, u32[]{:S(2)}, u32[]{:S(2)}) collective-permute-start(bf16[48,1536]{1,0:T(8,128)(2,1)S(1)} %collective-permute-done.3), channel_id=1, source_target_pairs={{0,256},{1,257},{2,258},{3,259},{4,260},{5,261},{6,262},{7,263},{8... | collective-permute-start | bytes 442376 | tf_op jit(solution)/shard_map/ppermute | solution.py:38
  79.9 3.1 %collective-permute-done.5 = bf16[48,1536]{1,0:T(8,128)(2,1)S(1)} collective-permute-done((bf16[48,1536]{1,0:T(8,128)(2,1)S(1)}, bf16[48,1536]{1,0:T(8,128)(2,1)S(1)}, u32[]{:S(2)}, u32[]{:S(2)}) %collective-permute-start.5) | collective-permute-done | bytes 147488 | tf_op jit(solution)/shard_map/ppermute | solution.py:38
  83.0 2.9 collective-permute-start.6
  85.9 4.9 %collective-permute-done.6 = bf16[48,1536]{1,0:T(8,128)(2,1)S(1)} collective-permute-done((bf16[48,1536]{1,0:T(8,128)(2,1)S(1)}, bf16[48,1536]{1,0:T(8,128)(2,1)S(1)}, u32[]{:S(2)}, u32[]{:S(2)}) %collective-permute-start.6) | collective-permute-done | bytes 147488 | tf_op jit(solution)/shard_map/ppermute | solution.py:38
  94.3 10.9 %collective-permute-done.18 = bf16[32,1536]{1,0:T(8,128)(2,1)} collective-permute-done((bf16[32,1536]{1,0:T(8,128)(2,1)}, bf16[32,1536]{1,0:T(8,128)(2,1)}, u32[]{:S(2)}, u32[]{:S(2)}) %collective-permute-start.18) | collective-permute-done | bytes 98336 | tf_op jit(solution)/shard_map/ppermute | solution.py:38
  107.7 6.1 %collective-permute-start.19 = (bf16[32,1536]{1,0:T(8,128)(2,1)}, bf16[32,1536]{1,0:T(8,128)(2,1)}, u32[]{:S(2)}, u32[]{:S(2)}) collective-permute-start(bf16[32,1536]{1,0:T(8,128)(2,1)} %collective-permute-done.18), channel_id=1, source_target_pairs={{0,16},{1,17},{2,18},{3,19},{4,20},{5,21},{6,22},{7,23},{8,24},{9,... | collective-permute-start | bytes 294920 | tf_op jit(solution)/shard_map/ppermute | solution.py:38
  113.8 16.7 %collective-permute-start.8 = (bf16[128,1536]{1,0:T(8,128)(2,1)S(1)}, bf16[128,1536]{1,0:T(8,128)(2,1)S(1)}, u32[]{:S(2)}, u32[]{:S(2)}) collective-permute-start(bf16[128,1536]{1,0:T(8,128)(2,1)S(1)} %slice.124), channel_id=1, source_target_pairs={{0,1},{1,0},{2,3},{3,2},{4,5},{5,4},{6,7},{7,6},{8,9},{9,8},{10,11... | collective-permute-start | bytes 1179656 | tf_op jit(solution)/shard_map/ppermute | solution.py:38
  145.6 20.8 %collective-permute-done.10 = bf16[1024,128]{0,1:T(8,128)(2,1)S(1)} collective-permute-done((bf16[1024,128]{0,1:T(8,128)(2,1)S(1)}, bf16[1024,128]{0,1:T(8,128)(2,1)S(1)}, u32[]{:S(2)}, u32[]{:S(2)}) %collective-permute-start.10) | collective-permute-done | bytes 262176 | tf_op jit(solution)/shard_map/ppermute | solution.py:38
  166.5 11.9 %collective-permute-start.11 = (bf16[1024,128]{0,1:T(8,128)(2,1)S(1)}, bf16[1024,128]{0,1:T(8,128)(2,1)S(1)}, u32[]{:S(2)}, u32[]{:S(2)}) collective-permute-start(bf16[1024,128]{0,1:T(8,128)(2,1)S(1)} %collective-permute-done.10), channel_id=1, source_target_pairs={{0,16},{1,17},{2,18},{3,19},{4,20},{5,21},{6,22},{7,23},{16,32},{1... | collective-permute-start | bytes 786440 | tf_op jit(solution)/shard_map/ppermute | solution.py:38
  180.5 3.7 %all-to-all-start.3 = ((bf16[4,64,1536]{2,1,0:T(8,128)(2,1)}), bf16[4,64,1536]{2,1,0:T(8,128)(2,1)S(1)}, u32[]{:S(2)}, u32[]{:S(2)}) async-start(bf16[4,64,1536]{2,1,0:T(8,128)(2,1)} %stack.138), calls=%async_computation.3 | async-start | bytes 1572864 | tf_op jit(solution)/shard_map/all_to_all | solution.py:18
  185.4 3.6 %fusion.118 = f32[2,512]{1,0:T(2,128)S(1)} fusion(pred[512,1536]{1,0:T(8,128)(4,1)} %compare_and_fusion, bf16[1024,64]{0,1:T(8,128)(2,1)S(1)} %get-tuple-element.10, bf16[1024,64]{0,1:T(8,128)(2,1)S(1)} %get-tuple-element.13, bf16[1,1024,64]{1,2,0:T(8,128)(2,1)} %get-tuple-element.9, bf16[1,1024,64]{1,2,0:T(8,128)(2,1)S(1)} %get-tuple-element.8), kind=kOutput, calls=%fused_computation.192 | convolution fusion | flops 208274944 | bytes 1314816 | tf_op jit(solution)/shard_map/sub | solution.py:102
  191.4 3.8 %fusion.20 = bf16[64,2,512]{2,0,1:T(8,128)(2,1)S(1)} fusion(f32[2,512]{1,0:T(2,128)S(1)} %fusion.121, pred[512,1536]{1,0:T(8,128)(4,1)S(1)} %copy-done.13, bf16[1024,64]{0,1:T(8,128)(2,1)S(1)} %get-tuple-element.12, bf16[1024,64]{0,1:T(8,128)(2,1)S(1)} %get-tuple-element.11, bf16[1024,64]{0,1:T(8,128)(2,1)S(1)} %get-tuple-element.13, ...), kind=kOutput, calls=%fused_computation.40 | convolution fusion | flops 411437568 | bytes 1708032 | tf_op jit(solution)/shard_map/hqk,kd->qhd/dot_general | solution.py:104
  195.2 4.0 %fusion.19 = bf16[64,2,512]{2,0,1:T(8,128)(2,1)S(1)} fusion(f32[2,512]{1,0:T(2,128)S(1)} %fusion.118, pred[512,1536]{1,0:T(8,128)(4,1)} %compare_and_fusion, bf16[1024,64]{0,1:T(8,128)(2,1)S(1)} %get-tuple-element.11, bf16[1024,64]{0,1:T(8,128)(2,1)S(1)} %get-tuple-element.12, bf16[1024,64]{0,1:T(8,128)(2,1)S(1)} %get-tuple-element.10, ...), kind=kOutput, calls=%fused_computation.39 | convolution fusion | flops 411634176 | bytes 1708032 | tf_op jit(solution)/shard_map/hqk,kd->qhd/dot_general | solution.py:104
  201.1 3.9 %all-to-all-start = ((bf16[8,256,128]{2,1,0:T(8,128)(2,1)}), bf16[8,256,128]{2,1,0:T(8,128)(2,1)S(1)}, u32[]{:S(2)}, u32[]{:S(2)}) async-start(bf16[8,256,128]{2,1,0:T(8,128)(2,1)} %pad_maximum_fusion.1), calls=%async_computation | async-start | bytes 1048576 | tf_op jit(solution)/shard_map/all_to_all | solution.py:175
  208.5 5.5 %collective-permute-done.17 = bf16[192,512]{1,0:T(8,128)(2,1)S(1)} collective-permute-done((bf16[192,512]{1,0:T(8,128)(2,1)}, bf16[192,512]{1,0:T(8,128)(2,1)S(1)}, u32[]{:S(2)}, u32[]{:S(2)}) %collective-permute-start.17) | collective-permute-done | bytes 196640 | tf_op jit(solution)/shard_map/ppermute | solution.py:38
  216.6 8.1 %all-to-all-start.2 = ((bf16[4,384,512]{2,1,0:T(8,128)(2,1)}), bf16[4,384,512]{2,1,0:T(8,128)(2,1)S(1)}, u32[]{:S(2)}, u32[]{:S(2)}) async-start(bf16[4,384,512]{2,1,0:T(8,128)(2,1)} %stack.137), calls=%async_computation.2 | async-start | bytes 3145728 | tf_op jit(solution)/shard_map/all_to_all | solution.py:18
  228.4 2.7 multiply_reduce_fusion
  232.7 11.5 %all-to-all-done.2 = bf16[4,384,512]{2,1,0:T(8,128)(2,1)S(1)} async-done(((bf16[4,384,512]{2,1,0:T(8,128)(2,1)}), bf16[4,384,512]{2,1,0:T(8,128)(2,1)S(1)}, u32[]{:S(2)}, u32[]{:S(2)}) %all-to-all-start.2) | async-done | bytes 1572896 | tf_op jit(solution)/shard_map/all_to_all | solution.py:18
  244.2 6.4 %all-to-all-start.1 = ((bf16[8,48,1536]{2,1,0:T(8,128)(2,1)}), bf16[8,48,1536]{2,1,0:T(8,128)(2,1)}, u32[]{:S(2)}, u32[]{:S(2)}) async-start(bf16[8,48,1536]{2,1,0:T(8,128)(2,1)} %bitcast.44), calls=%async_computation.1 | async-start | bytes 2359296 | tf_op jit(solution)/shard_map/all_to_all | solution.py:217
  250.6 2.9 bitcast_select_fusion
  260.9 6.3 %all-to-all-done.1 = bf16[8,48,1536]{2,1,0:T(8,128)(2,1)} async-done(((bf16[8,48,1536]{2,1,0:T(8,128)(2,1)}), bf16[8,48,1536]{2,1,0:T(8,128)(2,1)}, u32[]{:S(2)}, u32[]{:S(2)}) %all-to-all-start.1) | async-done | bytes 1179680 | tf_op jit(solution)/shard_map/all_to_all | solution.py:217
  267.2 2.6 fusion.126
  272.8 2.7 fusion.13
  275.5 4.5 %all-to-all-start.4 = ((bf16[8,48,1536]{2,1,0:T(8,128)(2,1)}), bf16[8,48,1536]{2,1,0:T(8,128)(2,1)S(1)}, u32[]{:S(2)}, u32[]{:S(2)}) async-start(bf16[8,48,1536]{2,1,0:T(8,128)(2,1)} %bitcast.51), calls=%async_computation.4 | async-start | bytes 2359296 | tf_op jit(solution)/shard_map/all_to_all | solution.py:228
  281.9 14.6 %all-to-all-done.4 = bf16[8,48,1536]{2,1,0:T(8,128)(2,1)S(1)} async-done(((bf16[8,48,1536]{2,1,0:T(8,128)(2,1)}), bf16[8,48,1536]{2,1,0:T(8,128)(2,1)S(1)}, u32[]{:S(2)}, u32[]{:S(2)}) %all-to-all-start.4) | async-done | bytes 1179680 | tf_op jit(solution)/shard_map/all_to_all | solution.py:228
  (181 shorter events, 82.5 us)
Async XLA Ops:
  7.2 23.0 %copy-start.27 = (s32[1,128]{1,0:T(1,128)S(1)}, s32[1,128]{1,0:T(1,128)}, u32[]{:S(2)}) copy-start(s32[1,128]{1,0:T(1,128)} %param.25) | copy-start | bytes 1540
  7.2 25.3 %copy-start.2 = (bf16[1536,256]{1,0:T(8,128)(2,1)S(1)}, bf16[1536,256]{1,0:T(8,128)(2,1)}, u32[]{:S(2)}) copy-start(bf16[1536,256]{1,0:T(8,128)(2,1)} %param.22) | copy-start | bytes 2359300
  7.2 221.2 %all-gather.2.cloned.1.call-start = ((), (), s32[]{:S(2)}) async-start(), calls=%async_computation.5 | async-start | bytes 3538944 | tf_op jit(solution)/shard_map/all_gather | solution.py:180
  10.4 97.3 %collective-permute-start = (bf16[128,1536]{1,0:T(8,128)(2,1)}, bf16[128,1536]{1,0:T(8,128)(2,1)}, u32[]{:S(2)}, u32[]{:S(2)}) collective-permute-start(bf16[128,1536]{1,0:T(8,128)(2,1)} %fusion.27), channel_id=1, source_target_pairs={{0,6},{1,7},{2,0},{3,1},{4,2},{5,3},{6,4},{7,5},{8,14},{9,15},{10,... | collective-permute-start | bytes 1179656 | tf_op jit(solution)/shard_map/ppermute | solution.py:38
  15.6 98.2 %collective-permute-start.1 = (bf16[128,1536]{1,0:T(8,128)(2,1)}, bf16[128,1536]{1,0:T(8,128)(2,1)}, u32[]{:S(2)}, u32[]{:S(2)}) collective-permute-start(bf16[128,1536]{1,0:T(8,128)(2,1)} %fusion.27), channel_id=1, source_target_pairs={{0,4},{1,5},{2,6},{3,7},{4,0},{5,1},{6,2},{7,3},{8,12},{9,13},{10,... | collective-permute-start | bytes 1179656 | tf_op jit(solution)/shard_map/ppermute | solution.py:38
  18.0 20.3 %collective-permute-start.12 = (s32[128]{0:T(128)}, s32[128]{0:T(128)}, u32[]{:S(2)}, u32[]{:S(2)}) collective-permute-start(s32[128]{0:T(128)} %param.19), channel_id=1, source_target_pairs={{0,6},{1,7},{2,0},{3,1},{4,2},{5,3},{6,4},{7,5},{8,14},{9,15},{10,... | collective-permute-start | bytes 1544 | tf_op jit(solution)/shard_map/ppermute | solution.py:38
  20.6 19.7 %collective-permute-start.13 = (s32[128]{0:T(128)}, s32[128]{0:T(128)}, u32[]{:S(2)}, u32[]{:S(2)}) collective-permute-start(s32[128]{0:T(128)} %param.19), channel_id=1, source_target_pairs={{0,4},{1,5},{2,6},{3,7},{4,0},{5,1},{6,2},{7,3},{8,12},{9,13},{10,... | collective-permute-start | bytes 1544 | tf_op jit(solution)/shard_map/ppermute | solution.py:38
  24.3 31.6 %collective-permute-start.14 = (s32[128]{0:T(128)}, s32[128]{0:T(128)}, u32[]{:S(2)}, u32[]{:S(2)}) collective-permute-start(s32[128]{0:T(128)} %param.19), channel_id=1, source_target_pairs={{0,2},{1,3},{2,4},{3,5},{4,6},{5,7},{6,0},{7,1},{8,10},{9,11},{10,... | collective-permute-start | bytes 1544 | tf_op jit(solution)/shard_map/ppermute | solution.py:38
  36.1 57.3 %copy-start.1 = (bf16[1536,512]{1,0:T(8,128)(2,1)}, bf16[1536,512]{1,0:T(8,128)(2,1)S(1)}, u32[]{:S(2)}) copy-start(bf16[1536,512]{1,0:T(8,128)(2,1)S(1)} %constant_dynamic-update-slice_fusion) | copy-start | bytes 4718596
  38.4 92.1 %collective-permute-start.2 = (bf16[128,1536]{1,0:T(8,128)(2,1)}, bf16[128,1536]{1,0:T(8,128)(2,1)}, u32[]{:S(2)}, u32[]{:S(2)}) collective-permute-start(bf16[128,1536]{1,0:T(8,128)(2,1)} %fusion.27), channel_id=1, source_target_pairs={{0,2},{1,3},{2,4},{3,5},{4,6},{5,7},{6,0},{7,1},{8,10},{9,11},{10,... | collective-permute-start | bytes 1179656 | tf_op jit(solution)/shard_map/ppermute | solution.py:38
  40.3 27.9 %collective-permute-start.3 = (bf16[48,1536]{1,0:T(8,128)(2,1)}, bf16[48,1536]{1,0:T(8,128)(2,1)S(1)}, u32[]{:S(2)}, u32[]{:S(2)}) collective-permute-start(bf16[48,1536]{1,0:T(8,128)(2,1)} %fusion.51), channel_id=1, source_target_pairs={{0,8},{1,9},{2,10},{3,11},{4,12},{5,13},{6,14},{7,15},{8,0},{9,1},... | collective-permute-start | bytes 442376 | tf_op jit(solution)/shard_map/ppermute | solution.py:38
  56.6 7.3 %collective-permute-start.15 = (s32[4,128]{1,0:T(4,128)S(1)}, s32[4,128]{1,0:T(4,128)S(1)}, u32[]{:S(2)}, u32[]{:S(2)}) collective-permute-start(s32[4,128]{1,0:T(4,128)S(1)} %get-tuple-element.19), channel_id=1, source_target_pairs={{0,1},{1,0},{2,3},{3,2},{4,5},{5,4},{6,7},{7,6},{8,9},{9,8},{10,11... | collective-permute-start | bytes 6152 | tf_op jit(solution)/shard_map/ppermute | solution.py:38
  64.0 68.6 %collective-permute-start.7 = (bf16[128,1536]{1,0:T(8,128)(2,1)}, bf16[128,1536]{1,0:T(8,128)(2,1)}, u32[]{:S(2)}, u32[]{:S(2)}) collective-permute-start(bf16[128,1536]{1,0:T(8,128)(2,1)} %pad_maximum_fusion.2), channel_id=1, source_target_pairs={{0,1},{1,0},{2,3},{3,2},{4,5},{5,4},{6,7},{7,6},{8,9},{9,8},{10,11... | collective-permute-start | bytes 1179656 | tf_op jit(solution)/shard_map/ppermute | solution.py:38
  68.3 7.3 %collective-permute-start.4 = (bf16[48,1536]{1,0:T(8,128)(2,1)S(1)}, bf16[48,1536]{1,0:T(8,128)(2,1)S(1)}, u32[]{:S(2)}, u32[]{:S(2)}) collective-permute-start(bf16[48,1536]{1,0:T(8,128)(2,1)S(1)} %collective-permute-done.3), channel_id=1, source_target_pairs={{0,384},{1,385},{2,386},{3,387},{4,388},{5,389},{6,390},{7,391},{8... | collective-permute-start | bytes 442376 | tf_op jit(solution)/shard_map/ppermute | solution.py:38
  75.6 7.4 %collective-permute-start.5 = (bf16[48,1536]{1,0:T(8,128)(2,1)S(1)}, bf16[48,1536]{1,0:T(8,128)(2,1)S(1)}, u32[]{:S(2)}, u32[]{:S(2)}) collective-permute-start(bf16[48,1536]{1,0:T(8,128)(2,1)S(1)} %collective-permute-done.3), channel_id=1, source_target_pairs={{0,256},{1,257},{2,258},{3,259},{4,260},{5,261},{6,262},{7,263},{8... | collective-permute-start | bytes 442376 | tf_op jit(solution)/shard_map/ppermute | solution.py:38
  83.0 7.8 %collective-permute-start.6 = (bf16[48,1536]{1,0:T(8,128)(2,1)S(1)}, bf16[48,1536]{1,0:T(8,128)(2,1)S(1)}, u32[]{:S(2)}, u32[]{:S(2)}) collective-permute-start(bf16[48,1536]{1,0:T(8,128)(2,1)S(1)} %collective-permute-done.3), channel_id=1, source_target_pairs={{0,128},{1,129},{2,130},{3,131},{4,132},{5,133},{6,134},{7,135},{8... | collective-permute-start | bytes 442376 | tf_op jit(solution)/shard_map/ppermute | solution.py:38
  90.8 14.5 %collective-permute-start.18 = (bf16[32,1536]{1,0:T(8,128)(2,1)}, bf16[32,1536]{1,0:T(8,128)(2,1)}, u32[]{:S(2)}, u32[]{:S(2)}) collective-permute-start(bf16[32,1536]{1,0:T(8,128)(2,1)} %constant_dynamic-slice_fusion), channel_id=1, source_target_pairs={{0,8},{1,9},{2,10},{3,11},{4,12},{5,13},{6,14},{7,15},{8,0},{9,1},... | collective-permute-start | bytes 294920 | tf_op jit(solution)/shard_map/ppermute | solution.py:38
  105.3 100.2 %collective-permute-start.16 = (bf16[192,512]{1,0:T(8,128)(2,1)}, bf16[192,512]{1,0:T(8,128)(2,1)}, u32[]{:S(2)}, u32[]{:S(2)}) collective-permute-start(bf16[192,512]{1,0:T(8,128)(2,1)} %constant_dynamic-slice_fusion.1), channel_id=1, source_target_pairs={{0,8},{1,9},{2,10},{3,11},{4,12},{5,13},{6,14},{7,15},{8,0},{9,1},... | collective-permute-start | bytes 589832 | tf_op jit(solution)/shard_map/ppermute | solution.py:38
  107.7 70.7 %collective-permute-start.19 = (bf16[32,1536]{1,0:T(8,128)(2,1)}, bf16[32,1536]{1,0:T(8,128)(2,1)}, u32[]{:S(2)}, u32[]{:S(2)}) collective-permute-start(bf16[32,1536]{1,0:T(8,128)(2,1)} %collective-permute-done.18), channel_id=1, source_target_pairs={{0,16},{1,17},{2,18},{3,19},{4,20},{5,21},{6,22},{7,23},{8,24},{9,... | collective-permute-start | bytes 294920 | tf_op jit(solution)/shard_map/ppermute | solution.py:38
  113.8 20.5 %collective-permute-start.8 = (bf16[128,1536]{1,0:T(8,128)(2,1)S(1)}, bf16[128,1536]{1,0:T(8,128)(2,1)S(1)}, u32[]{:S(2)}, u32[]{:S(2)}) collective-permute-start(bf16[128,1536]{1,0:T(8,128)(2,1)S(1)} %slice.124), channel_id=1, source_target_pairs={{0,1},{1,0},{2,3},{3,2},{4,5},{5,4},{6,7},{7,6},{8,9},{9,8},{10,11... | collective-permute-start | bytes 1179656 | tf_op jit(solution)/shard_map/ppermute | solution.py:38
  134.9 3.4 %collective-permute-start.9 = (bf16[512,256]{0,1:T(8,128)(2,1)S(1)}, bf16[512,256]{0,1:T(8,128)(2,1)S(1)}, u32[]{:S(2)}, u32[]{:S(2)}) collective-permute-start(bf16[512,256]{0,1:T(8,128)(2,1)S(1)} %pad_maximum_fusion.5), channel_id=1, source_target_pairs={{0,1},{1,0},{2,3},{3,2},{4,5},{5,4},{6,7},{7,6},{8,9},{9,8},{10,11... | collective-permute-start | bytes 786440 | tf_op jit(solution)/shard_map/ppermute | solution.py:38
  141.7 47.3 %copy-start.17 = (bf16[1,1024,64]{1,2,0:T(8,128)(2,1)}, bf16[1,1024,64]{1,2,0:T(8,128)(2,1)S(1)}, u32[]{:S(2)}) copy-start(bf16[1,1024,64]{1,2,0:T(8,128)(2,1)S(1)} %get-tuple-element.8) | copy-start | bytes 393220
  141.8 24.7 %collective-permute-start.10 = (bf16[1024,128]{0,1:T(8,128)(2,1)S(1)}, bf16[1024,128]{0,1:T(8,128)(2,1)S(1)}, u32[]{:S(2)}, u32[]{:S(2)}) collective-permute-start(bf16[1024,128]{0,1:T(8,128)(2,1)S(1)} %get-tuple-element.15), channel_id=1, source_target_pairs={{0,8},{1,9},{2,10},{3,11},{4,12},{5,13},{6,14},{7,15},{8,0},{9,1},... | collective-permute-start | bytes 786440 | tf_op jit(solution)/shard_map/ppermute | solution.py:38
  166.5 18.8 %collective-permute-start.11 = (bf16[1024,128]{0,1:T(8,128)(2,1)S(1)}, bf16[1024,128]{0,1:T(8,128)(2,1)S(1)}, u32[]{:S(2)}, u32[]{:S(2)}) collective-permute-start(bf16[1024,128]{0,1:T(8,128)(2,1)S(1)} %collective-permute-done.10), channel_id=1, source_target_pairs={{0,16},{1,17},{2,18},{3,19},{4,20},{5,21},{6,22},{7,23},{16,32},{1... | collective-permute-start | bytes 786440 | tf_op jit(solution)/shard_map/ppermute | solution.py:38
  180.5 20.7 %all-to-all-start.3 = ((bf16[4,64,1536]{2,1,0:T(8,128)(2,1)}), bf16[4,64,1536]{2,1,0:T(8,128)(2,1)S(1)}, u32[]{:S(2)}, u32[]{:S(2)}) async-start(bf16[4,64,1536]{2,1,0:T(8,128)(2,1)} %stack.138), calls=%async_computation.3 | async-start | bytes 1572864 | tf_op jit(solution)/shard_map/all_to_all | solution.py:18
  201.1 14.1 %all-to-all-start = ((bf16[8,256,128]{2,1,0:T(8,128)(2,1)}), bf16[8,256,128]{2,1,0:T(8,128)(2,1)S(1)}, u32[]{:S(2)}, u32[]{:S(2)}) async-start(bf16[8,256,128]{2,1,0:T(8,128)(2,1)} %pad_maximum_fusion.1), calls=%async_computation | async-start | bytes 1048576 | tf_op jit(solution)/shard_map/all_to_all | solution.py:175
  205.5 8.6 %collective-permute-start.17 = (bf16[192,512]{1,0:T(8,128)(2,1)}, bf16[192,512]{1,0:T(8,128)(2,1)S(1)}, u32[]{:S(2)}, u32[]{:S(2)}) collective-permute-start(bf16[192,512]{1,0:T(8,128)(2,1)} %collective-permute-done.16), channel_id=1, source_target_pairs={{0,16},{1,17},{2,18},{3,19},{4,20},{5,21},{6,22},{7,23},{8,24},{9,... | collective-permute-start | bytes 589832 | tf_op jit(solution)/shard_map/ppermute | solution.py:38
  216.6 27.6 %all-to-all-start.2 = ((bf16[4,384,512]{2,1,0:T(8,128)(2,1)}), bf16[4,384,512]{2,1,0:T(8,128)(2,1)S(1)}, u32[]{:S(2)}, u32[]{:S(2)}) async-start(bf16[4,384,512]{2,1,0:T(8,128)(2,1)} %stack.137), calls=%async_computation.2 | async-start | bytes 3145728 | tf_op jit(solution)/shard_map/all_to_all | solution.py:18
  244.2 23.0 %all-to-all-start.1 = ((bf16[8,48,1536]{2,1,0:T(8,128)(2,1)}), bf16[8,48,1536]{2,1,0:T(8,128)(2,1)}, u32[]{:S(2)}, u32[]{:S(2)}) async-start(bf16[8,48,1536]{2,1,0:T(8,128)(2,1)} %bitcast.44), calls=%async_computation.1 | async-start | bytes 2359296 | tf_op jit(solution)/shard_map/all_to_all | solution.py:217
  253.4 16.9 %collective-permute-start.20 = (bf16[1536,512]{1,0:T(8,128)(2,1)}, bf16[1536,512]{1,0:T(8,128)(2,1)}, u32[]{:S(2)}, u32[]{:S(2)}) collective-permute-start(bf16[1536,512]{1,0:T(8,128)(2,1)} %bitcast_select_fusion), channel_id=1, source_target_pairs={{0,1},{1,0},{2,3},{3,2},{4,5},{5,4},{6,7},{7,6},{8,9},{9,8},{10,11... | collective-permute-start | bytes 4718600 | tf_op jit(solution)/shard_map/ppermute | solution.py:38
  256.9 16.0 %collective-permute-start.21 = (bf16[256,1536]{1,0:T(8,128)(2,1)}, bf16[256,1536]{1,0:T(8,128)(2,1)}, u32[]{:S(2)}, u32[]{:S(2)}) collective-permute-start(bf16[256,1536]{1,0:T(8,128)(2,1)} %get-tuple-element.4), channel_id=1, source_target_pairs={{0,1},{1,0},{2,3},{3,2},{4,5},{5,4},{6,7},{7,6},{8,9},{9,8},{10,11... | collective-permute-start | bytes 2359304 | tf_op jit(solution)/shard_map/ppermute | solution.py:38
  275.5 21.0 %all-to-all-start.4 = ((bf16[8,48,1536]{2,1,0:T(8,128)(2,1)}), bf16[8,48,1536]{2,1,0:T(8,128)(2,1)S(1)}, u32[]{:S(2)}, u32[]{:S(2)}) async-start(bf16[8,48,1536]{2,1,0:T(8,128)(2,1)} %bitcast.51), calls=%async_computation.4 | async-start | bytes 2359296 | tf_op jit(solution)/shard_map/all_to_all | solution.py:228
  (24 other events, 134.4 us)
Sparse Core Ops, SparseCore 0:
  94.5 42.0 all-gather.1
